TPU v7x, 512 devices: a whole 4x8x8 slice. The times are simulated.
512 devices in a mesh: band: 8 (over y), gy: 8 (over z), gz: 8 (over x, core).
Axes of the slice: x: 4, y: 8, z: 8, core: 2. Of those that a mesh axis runs over, the one named last changes fastest.
Arguments:
- orbitals: float32 [1024, 48, 3840], P('band', 'gy', 'gz'), may hold values from -6 to 6
- occupied: bfloat16 [1024, 48, 3840], P('band', 'gy', 'gz'), may hold values from -6 to 6
- eigen: float32 [1024], P('band'), may hold values from -1.5 to 0
- potential: float32 [48, 3840], P('gy', 'gz'), may hold values from -2 to 0.5
- perturbation: float32 [48, 3840], P('gy', 'gz'), may hold values from 0.2 to 1.5
- precondition: float32 [48, 3840], P('gy', 'gz'), may hold values from 0.05 to 0.3
Outputs:
- updated: float32 [1024, 48, 3840], P('band', 'gy', 'gz')
- resid_norm: float32 [1024], P('band')
All inputs are finite; a program needn't handle non-finite values.
Results may differ from a plain program's by a relative error of at most 0.0008.
Values may be sent and summed in bfloat16 or wider, within the bound.
A program may use at most 128 MiB of HBM per device.

v0:
```python
import jax
import jax.numpy as jnp
from jax import lax
from jax.sharding import PartitionSpec as P

NX = 80
stencil = (-205.0 / 72.0, 8.0 / 5.0, -1.0 / 5.0, 8.0 / 315.0, -1.0 / 560.0)


def extended(block, sides, width):
    for axis, dim in sides:
        count = lax.axis_size(axis)
        forward = [(i, i + 1) for i in range(count - 1)]
        forward.append((count - 1, 0))
        backward = [(target, source) for source, target in forward]
        low = lax.ppermute(
            lax.slice_in_dim(block, block.shape[dim] - width, None, axis=dim), axis, forward
        )
        high = lax.ppermute(lax.slice_in_dim(block, 0, width, axis=dim), axis, backward)
        block = jnp.concatenate([low, block, high], axis=dim)
    return block


def along_x(field, dist):
    flat = field.shape[-1]
    position = lax.broadcasted_iota(jnp.int32, (flat,), 0) % NX
    lower = jnp.where(position >= dist, jnp.roll(field, dist, -1), jnp.roll(field, dist - NX, -1))
    upper = jnp.where(
        position < NX - dist, jnp.roll(field, -dist, -1), jnp.roll(field, NX - dist, -1)
    )
    return lower + upper


def laplace(field):
    rows_y = field.shape[1]
    flat = field.shape[2]
    padded_y = extended(field, (("gy", 1),), 4)
    padded_z = extended(field, (("gz", 2),), 4 * NX)
    total = 3.0 * stencil[0] * field
    for dist in range(1, 5):
        pair_y = (
            padded_y[:, 4 + dist : 4 + dist + rows_y, :]
            + padded_y[:, 4 - dist : 4 - dist + rows_y, :]
        )
        pair_z = (
            padded_z[:, :, (4 + dist) * NX : (4 + dist) * NX + flat]
            + padded_z[:, :, (4 - dist) * NX : (4 - dist) * NX + flat]
        )
        total = total + stencil[dist] * (along_x(field, dist) + pair_y + pair_z)
    return total


def on_device(orbitals, occupied, eigen, potential, perturbation, precondition):
    band_rows, rows_y, flat = orbitals.shape
    cells = NX * rows_y * lax.axis_size("gy") * (flat // NX) * lax.axis_size("gz")
    occ_wide = occupied.astype(jnp.float32)
    resid = (
        -0.5 * laplace(orbitals)
        + (potential[None] - eigen[:, None, None]) * orbitals
        + perturbation[None] * occ_wide
    )
    squares = jnp.sum(resid * resid, axis=(1, 2))
    squares = lax.psum(squares, ("gy", "gz"))
    trial = orbitals - precondition[None] * resid
    trial_low = trial.astype(jnp.bfloat16)
    partial_margins = jnp.einsum(
        "oyc,ryc->or",
        lax.all_gather(occupied, "band", axis=0, tiled=True),
        trial_low,
        preferred_element_type=jnp.float32,
    )
    margins = lax.psum(partial_margins, ("gy", "gz"))
    norms = jnp.sqrt(squares / cells + 1e-06)
    coeff = (margins / cells).astype(jnp.bfloat16)
    correction = jnp.einsum(
        "or,oyc->ryc",
        coeff,
        lax.all_gather(occupied, "band", axis=0, tiled=True),
        preferred_element_type=jnp.float32,
    )
    updated = trial - correction
    return (updated, norms)


def solution(mesh):
    placed = (
        P("band", "gy", "gz"),
        P("band", "gy", "gz"),
        P("band"),
        P("gy", "gz"),
        P("gy", "gz"),
        P("gy", "gz"),
    )
    return jax.shard_map(
        on_device,
        mesh=mesh,
        in_specs=placed,
        out_specs=(P("band", "gy", "gz"), P("band")),
        check_vma=False,
    )
```

profile of v0, /device:TPU:8, one launch (start us, length us, event | category | flops | bytes accessed | tf_op | source)
XLA Modules:
  0.0 306.1 jit_solution(4770405374905059568)
XLA Ops:
  7.2 0.0 all-gather.2.cloned.1.call-start
  7.2 0.7 all-gather.2.cloned.1.call-update
  7.9 0.0 copy-start
  7.9 0.0 all-reduce.2.cloned.1.call-start
  8.0 1.7 fusion.56
  9.7 4.3 %collective-permute-start.1 = (f32[128,4,480]{0,2,1:T(8,128)S(1)}, f32[128,4,480]{0,2,1:T(8,128)S(1)}, u32[]{:S(2)}, u32[]{:S(2)}) collective-permute-start(f32[128,4,480]{0,2,1:T(8,128)S(1)} %get-tuple-element.37), channel_id=1, source_target_pairs={{0,8},{8,16},{16,24},{24,32},{32,40},{40,48},{48,56},{56,0},{1,9},... | collective-permute-start | bytes 2949128 | tf_op jit(solution)/shard_map/ppermute | solution.py:16
  14.0 0.0 copy-done
  14.0 0.2 fusion.57
  14.2 0.0 collective-permute-start.3
  14.2 8.6 %collective-permute-start = (f32[128,4,480]{0,2,1:T(8,128)S(1)}, f32[128,4,480]{0,2,1:T(8,128)S(1)}, u32[]{:S(2)}, u32[]{:S(2)}) collective-permute-start(f32[128,4,480]{0,2,1:T(8,128)S(1)} %get-tuple-element.36), channel_id=1, source_target_pairs={{8,0},{16,8},{24,16},{32,24},{40,32},{48,40},{56,48},{0,56},{9,1},... | collective-permute-start | bytes 2949128 | tf_op jit(solution)/shard_map/ppermute | solution.py:19
  22.8 2.7 collective-permute-start.2
  25.4 0.6 fusion.40
  26.1 0.8 fusion.47
  27.0 0.8 fusion.51
  27.8 0.9 fusion.55
  28.7 1.2 fusion.46
  29.9 1.6 fusion.50
  31.5 1.9 fusion.45
  33.4 1.9 fusion.49
  35.3 1.8 fusion.53
  37.1 1.8 fusion.41
  38.9 0.5 fusion.29
  39.4 0.6 fusion.31
  40.0 1.6 fusion.54
  41.6 0.6 fusion.33
  42.2 0.5 fusion.35
  42.7 1.6 fusion.42
  44.4 0.0 collective-permute-done.1
  44.4 0.1 constant_dynamic-update-slice_fusion.3
  44.4 0.0 collective-permute-done.3
  44.5 0.1 constant_dynamic-update-slice_fusion.7
  44.5 0.6 constant_dynamic-update-slice_fusion.1
  45.2 0.0 collective-permute-done
  45.2 0.1 constant_dynamic-update-slice_fusion
  45.2 0.0 copy-start.2
  45.3 0.0 copy-start.3
  45.3 0.0 collective-permute-done.2
  45.3 0.1 constant_dynamic-update-slice_fusion.4
  45.4 0.6 copy-done.2
  46.0 0.0 copy-done.3
  46.0 13.7 %multiply_reduce_fusion = (f32[128]{0:T(128)}, f32[128,6,480]{0,2,1:T(8,128)S(1)}) fusion(bf16[128,6,480]{0,2,1:T(8,128)(2,1)} %param.7, f32[6,480]{1,0:T(8,128)S(1)} %copy-done.2, f32[128,6,480]{0,2,1:T(8,128)S(1)} %copy-done, f32[128]{0:T(128)} %param.8, f32[6,480]{1,0:T(8,128)S(1)} %copy-done.3, f32[128,6,800]{0,2,1:T(8,128)S(1)} %get-tuple-element.39, ...), kind=kLoop, calls=%fused_computation.39 | loop fusion | flops 22855552 | bytes 50900224 | tf_op jit(solution)/shard_map/reduce_sum | solution.py:62
  59.7 35.2 %all-gather.2.cloned.1.call-done = bf16[1024,6,480]{0,2,1:T(8,128)(2,1)} async-done(((bf16[128,6,480]{0,2,1:T(8,128)(2,1)}), bf16[1024,6,480]{0,2,1:T(8,128)(2,1)}) %all-gather.2.cloned.1.call-update) | async-done | bytes 5898256 | tf_op jit(solution)/shard_map/all_gather | solution.py:68
  94.9 6.2 %convolution_bitcast_fusion = f32[1024,128]{1,0:T(8,128)} fusion(bf16[1024,6,480]{0,2,1:T(8,128)(2,1)} %all-gather.2.cloned.1.call-done, f32[128,6,480]{0,2,1:T(8,128)S(1)} %copy-done, f32[128,6,480]{0,2,1:T(8,128)S(1)} %get-tuple-element.3, f32[6,480]{1,0:T(8,128)S(1)} %copy-done.1), kind=kOutput, calls=%fused_computation.42 | convolution fusion | flops 756080640 | bytes 9383168 | tf_op jit(solution)/shard_map/oyc,ryc->or/dot_general | solution.py:66
  101.1 0.0 all-reduce.2.cloned.1.call-update
  101.1 125.7 %psum.15 = f32[128]{0:T(128)S(1)} all-reduce(f32[128]{0:T(128)S(1)} %copy-done.4), channel_id=1, replica_groups=mesh['band'=8,'gy'=8,'gz'=8] {'gy','gz'}, use_global_device_ids=true, to_apply=%region_2.3 | all-reduce | flops 128 | bytes 1024 | tf_op jit(solution)/shard_map/psum | solution.py:63
  226.8 0.5 add_sqrt_fusion
  227.3 66.2 %all-reduce.2.cloned.1.call-done = f32[1024,128]{1,0:T(8,128)} async-done(((f32[1024,128]{1,0:T(8,128)}), f32[1024,128]{1,0:T(8,128)}) %all-reduce.2.cloned.1.call-update) | async-done | bytes 524304 | tf_op jit(solution)/shard_map/psum | solution.py:72
  293.6 5.7 %convolution_subtract_fusion = f32[128,6,480]{0,2,1:T(8,128)} fusion(bf16[1024,6,480]{0,2,1:T(8,128)(2,1)} %all-gather.2.cloned.1.call-done, f32[128,6,480]{0,2,1:T(8,128)S(1)} %copy-done, f32[128,6,480]{0,2,1:T(8,128)S(1)} %get-tuple-element.3, f32[6,480]{1,0:T(8,128)S(1)} %copy-done.1, f32[1024,128]{1,0:T(8,128)} %all-reduce.2.cloned.1.call-done), kind=kOutput, calls=%fused_computation.41 | convolution fusion | flops 756342784 | bytes 10857728 | tf_op jit(solution)/shard_map/or,oyc->ryc/dot_general | solution.py:75
  (8 shorter events, 0.1 us)
Async XLA Ops:
  7.2 87.7 %all-gather.2.cloned.1.call-start = ((), (), s32[]{:S(2)}) async-start(), calls=%async_computation | async-start | bytes 6635520 | tf_op jit(solution)/shard_map/all_gather | solution.py:68
  7.9 6.1 %copy-start = (f32[128,6,480]{0,2,1:T(8,128)S(1)}, f32[128,6,480]{0,2,1:T(8,128)}, u32[]{:S(2)}) copy-start(f32[128,6,480]{0,2,1:T(8,128)} %param.6) | copy-start | bytes 4423684
  7.9 285.7 %all-reduce.2.cloned.1.call-start = ((), (), s32[]{:S(2)}) async-start(), calls=%async_computation.1 | async-start | bytes 1048576 | tf_op jit(solution)/shard_map/psum | solution.py:72
  9.7 34.7 %collective-permute-start.1 = (f32[128,4,480]{0,2,1:T(8,128)S(1)}, f32[128,4,480]{0,2,1:T(8,128)S(1)}, u32[]{:S(2)}, u32[]{:S(2)}) collective-permute-start(f32[128,4,480]{0,2,1:T(8,128)S(1)} %get-tuple-element.37), channel_id=1, source_target_pairs={{0,8},{8,16},{16,24},{24,32},{32,40},{40,48},{48,56},{56,0},{1,9},... | collective-permute-start | bytes 2949128 | tf_op jit(solution)/shard_map/ppermute | solution.py:16
  14.2 30.3 %collective-permute-start.3 = (f32[128,6,320]{0,2,1:T(8,128)S(1)}, f32[128,6,320]{0,2,1:T(8,128)S(1)}, u32[]{:S(2)}, u32[]{:S(2)}) collective-permute-start(f32[128,6,320]{0,2,1:T(8,128)S(1)} %get-tuple-element.43), channel_id=1, source_target_pairs={{0,1},{1,2},{2,3},{3,4},{4,5},{5,6},{6,7},{7,0},{8,9},{9,10},{10,1... | collective-permute-start | bytes 2949128 | tf_op jit(solution)/shard_map/ppermute | solution.py:16
  14.2 31.0 %collective-permute-start = (f32[128,4,480]{0,2,1:T(8,128)S(1)}, f32[128,4,480]{0,2,1:T(8,128)S(1)}, u32[]{:S(2)}, u32[]{:S(2)}) collective-permute-start(f32[128,4,480]{0,2,1:T(8,128)S(1)} %get-tuple-element.36), channel_id=1, source_target_pairs={{8,0},{16,8},{24,16},{32,24},{40,32},{48,40},{56,48},{0,56},{9,1},... | collective-permute-start | bytes 2949128 | tf_op jit(solution)/shard_map/ppermute | solution.py:19
  22.8 22.5 %collective-permute-start.2 = (f32[128,6,320]{0,2,1:T(8,128)S(1)}, f32[128,6,320]{0,2,1:T(8,128)S(1)}, u32[]{:S(2)}, u32[]{:S(2)}) collective-permute-start(f32[128,6,320]{0,2,1:T(8,128)S(1)} %get-tuple-element.42), channel_id=1, source_target_pairs={{1,0},{2,1},{3,2},{4,3},{5,4},{6,5},{7,6},{0,7},{9,8},{10,9},{11,1... | collective-permute-start | bytes 2949128 | tf_op jit(solution)/shard_map/ppermute | solution.py:19
  45.2 0.7 copy-start.2
  45.3 0.7 copy-start.3
  46.0 48.9 %copy-start.1 = (f32[6,480]{1,0:T(8,128)S(1)}, f32[6,480]{1,0:T(8,128)}, u32[]{:S(2)}) copy-start(f32[6,480]{1,0:T(8,128)} %param.11) | copy-start | bytes 34564
  94.9 6.3 %copy-start.4 = (f32[128]{0:T(128)S(1)}, f32[128]{0:T(128)}, u32[]{:S(2)}) copy-start(f32[128]{0:T(128)} %get-tuple-element.2) | copy-start | bytes 1540
Sparse Core Ops, SparseCore 0:
  10.0 84.8 all-gather.1
  101.2 192.2 all-reduce.1
where the time goes:
time: 306 us
  blocking collectives  126 us (41%)
  waiting for transfers between devices  102 us (33%)
  local copies, waits for them, and re-layouts  20.1 us (7%)
  other arithmetic  16.5 us (5%)
  starting transfers between devices  15.6 us (5%)
  between operations  14.2 us (5%)
  matrix products  11.9 us (4%)
    psum x1, blocking collectives, on_device(): squares = lax.psum(squares, ('gy', 'gz'))  126 us
    psum x1, waiting for transfers between devices, on_device(): margins = lax.psum(partial_margins, ('gy', 'gz'))  66.2 us
    all_gather x1, waiting for transfers between devices, on_device(): lax.all_gather(occupied, 'band', axis=0, tiled=True)  35.2 us
    reduce_sum x1, other arithmetic, on_device(): squares = jnp.sum(resid * resid, axis=(1, 2))  13.7 us
    ppermute x2, starting transfers between devices, extended(): lax.ppermute(lax.slice_in_dim(block, 0, width, axis=dim), axis, backward)  11.2 us
    slice x8, local copies, waits for them, and re-layouts, along_x(): jnp.roll(field, dist - NX, -1)  8.63 us
    slice x8, local copies, waits for them, and re-layouts, along_x(): jnp.roll(field, dist, -1)  8.03 us
    dot_general x1, matrix products, on_device(): jnp.einsum('oyc,ryc->or', lax.all_gather(occupied, 'band', axis=0, tiled=...  6.24 us
  transfers between devices with their start and end apart: 6, of which 2 were waited for; matrix products, arithmetic and copies ran while one was open for 12% of the time, Pallas kernels for 0%

commit v1 on v0

--- a/solution.py
+++ b/solution.py
@@ -69,7 +69,7 @@
         trial_low,
         preferred_element_type=jnp.float32,
     )
-    margins = lax.psum(partial_margins, ("gy", "gz"))
+    margins = jnp.sum(lax.all_gather(partial_margins, ("gy", "gz")), axis=0)
     norms = jnp.sqrt(squares / cells + 1e-06)
     coeff = (margins / cells).astype(jnp.bfloat16)
     correction = jnp.einsum(

time: 306 us -> 297 us (0.971)
  the two profiles are of different devices: /device:TPU:8 before, /device:TPU:1 now
where the time goes in v1:
time: 297 us
  blocking collectives  131 us (44%)
  waiting for transfers between devices  54.6 us (18%)
  local copies, waits for them, and re-layouts  48 us (16%)
  other arithmetic  23.2 us (8%)
  starting transfers between devices  15.3 us (5%)
  between operations  14.2 us (5%)
  matrix products  10.7 us (4%)
    psum x1, blocking collectives, on_device(): squares = lax.psum(squares, ('gy', 'gz'))  131 us
    unnamed x14, local copies, waits for them, and re-layouts  29.6 us
    all_gather x1, waiting for transfers between devices, on_device(): lax.all_gather(occupied, 'band', axis=0, tiled=True)  29 us
    all_gather x1, waiting for transfers between devices, on_device(): margins = jnp.sum(lax.all_gather(partial_margins, ('gy', 'gz')), axis=0)  20.6 us
    reduce_sum x1, other arithmetic, on_device(): squares = jnp.sum(resid * resid, axis=(1, 2))  13.6 us
    ppermute x2, starting transfers between devices, extended(): lax.ppermute(lax.slice_in_dim(block, 0, width, axis=dim), axis, backward)  13.3 us
    slice x8, local copies, waits for them, and re-layouts, along_x(): jnp.roll(field, dist - NX, -1)  8.5 us
    slice x8, local copies, waits for them, and re-layouts, along_x(): jnp.roll(field, dist, -1)  7.91 us
  transfers between devices with their start and end apart: 6, of which 3 were waited for; matrix products, arithmetic and copies ran while one was open for 12% of the time, Pallas kernels for 0%

profile of v1, /device:TPU:1, one launch (start us, length us, event | category | flops | bytes accessed | tf_op | source)
XLA Modules:
  0.0 296.6 jit_solution(7964956942114754367)
XLA Ops:
  7.2 0.0 all-gather.4.cloned.1.call-start
  7.2 0.7 all-gather.4.cloned.1.call-update
  7.9 0.0 all-gather.6.cloned.1.call-start
  8.0 1.7 fusion.57
  9.7 6.9 %collective-permute-start.2 = (f32[128,6,320]{0,2,1:T(8,128)S(1)}, f32[128,6,320]{0,2,1:T(8,128)S(1)}, u32[]{:S(2)}, u32[]{:S(2)}) collective-permute-start(f32[128,6,320]{0,2,1:T(8,128)S(1)} %get-tuple-element.42), channel_id=1, source_target_pairs={{1,0},{2,1},{3,2},{4,3},{5,4},{6,5},{7,6},{0,7},{9,8},{10,9},{11,1... | collective-permute-start | bytes 2949128 | tf_op jit(solution)/shard_map/ppermute | solution.py:19
  16.6 0.0 collective-permute-start.3
  16.6 0.1 fusion.56
  16.7 6.4 %collective-permute-start = (f32[128,4,480]{0,2,1:T(8,128)S(1)}, f32[128,4,480]{0,2,1:T(8,128)S(1)}, u32[]{:S(2)}, u32[]{:S(2)}) collective-permute-start(f32[128,4,480]{0,2,1:T(8,128)S(1)} %get-tuple-element.36), channel_id=1, source_target_pairs={{8,0},{16,8},{24,16},{32,24},{40,32},{48,40},{56,48},{0,56},{9,1},... | collective-permute-start | bytes 2949128 | tf_op jit(solution)/shard_map/ppermute | solution.py:19
  23.2 1.9 collective-permute-start.1
  25.1 0.6 fusion.40
  25.8 0.8 fusion.51
  26.6 0.8 fusion.47
  27.4 0.8 fusion.43
  28.3 1.2 fusion.46
  29.4 1.6 fusion.54
  31.1 1.8 fusion.45
  32.9 1.8 fusion.49
  34.7 1.9 fusion.41
  36.5 1.8 fusion.53
  38.4 0.5 fusion.35
  38.9 0.6 fusion.33
  39.5 1.6 fusion.50
  41.0 0.6 fusion.31
  41.6 0.6 fusion.29
  42.2 1.6 fusion.42
  43.8 0.0 collective-permute-done.3
  43.9 0.1 constant_dynamic-update-slice_fusion.7
  43.9 4.3 %collective-permute-done.1 = f32[128,4,480]{0,2,1:T(8,128)S(1)} collective-permute-done((f32[128,4,480]{0,2,1:T(8,128)S(1)}, f32[128,4,480]{0,2,1:T(8,128)S(1)}, u32[]{:S(2)}, u32[]{:S(2)}) %collective-permute-start.1) | collective-permute-done | bytes 983072 | tf_op jit(solution)/shard_map/ppermute | solution.py:16
  48.3 0.1 constant_dynamic-update-slice_fusion.3
  48.3 0.6 constant_dynamic-update-slice_fusion.1
  49.0 0.0 collective-permute-done
  49.0 0.1 constant_dynamic-update-slice_fusion
  49.0 0.0 copy-start.2
  49.1 0.0 copy-start.3
  49.1 0.0 collective-permute-done.2
  49.1 0.1 constant_dynamic-update-slice_fusion.4
  49.1 0.6 copy-done.2
  49.8 0.0 copy-done.3
  49.8 13.6 %multiply_reduce_fusion = (f32[128]{0:T(128)}, f32[128,6,480]{0,2,1:T(8,128)S(1)}) fusion(bf16[128,6,480]{0,2,1:T(8,128)(2,1)} %param.7, f32[6,480]{1,0:T(8,128)S(1)} %copy-done.2, f32[128,6,480]{0,2,1:T(8,128)S(1)} %copy-done, f32[128]{0:T(128)} %param.8, f32[6,480]{1,0:T(8,128)S(1)} %copy-done.3, f32[128,6,800]{0,2,1:T(8,128)S(1)} %get-tuple-element.39, ...), kind=kLoop, calls=%fused_computation.40 | loop fusion | flops 22855552 | bytes 50900224 | tf_op jit(solution)/shard_map/reduce_sum | solution.py:62
  63.4 29.0 %all-gather.4.cloned.1.call-done = bf16[1024,6,480]{0,2,1:T(8,128)(2,1)} async-done(((bf16[128,6,480]{0,2,1:T(8,128)(2,1)}), bf16[1024,6,480]{0,2,1:T(8,128)(2,1)}) %all-gather.4.cloned.1.call-update) | async-done | bytes 5898256 | tf_op jit(solution)/shard_map/all_gather | solution.py:68
  92.4 5.2 %convolution_bitcast_fusion = f32[1024,128]{0,1:T(8,128)} fusion(bf16[1024,6,480]{0,2,1:T(8,128)(2,1)} %all-gather.4.cloned.1.call-done, f32[128,6,480]{0,2,1:T(8,128)S(1)} %copy-done, f32[128,6,480]{0,2,1:T(8,128)S(1)} %get-tuple-element.3, f32[6,480]{1,0:T(8,128)S(1)} %copy-done.1), kind=kOutput, calls=%fused_computation.43 | convolution fusion | flops 756080640 | bytes 9383168 | tf_op jit(solution)/shard_map/oyc,ryc->or/dot_general | solution.py:66
  97.6 0.0 all-gather.6.cloned.1.call-update
  97.6 130.6 %psum.7 = f32[128]{0:T(128)S(1)} all-reduce(f32[128]{0:T(128)S(1)} %copy-done.4), channel_id=1, replica_groups=mesh['band'=8,'gy'=8,'gz'=8] {'gy','gz'}, use_global_device_ids=true, to_apply=%region_2.3 | all-reduce | flops 128 | bytes 1024 | tf_op jit(solution)/shard_map/psum | solution.py:63
  228.2 0.5 add_sqrt_fusion
  228.7 20.6 %all-gather.6.cloned.1.call-done = f32[65536,128]{0,1:T(8,128)} async-done(((f32[1024,128]{0,1:T(8,128)}), f32[65536,128]{0,1:T(8,128)}) %all-gather.6.cloned.1.call-update) | async-done | bytes 33554448 | tf_op jit(solution)/shard_map/all_gather | solution.py:72
  249.3 28.2 %copy.11 = f32[16,8,64,1024]{3,2,1,0:T(8,128)S(1)} copy(f32[16,8,64,1024]{3,1,2,0:T(8,128)} %bitcast.14) | data formatting | bytes 67108864
  277.6 6.7 %bitcast_reduce_fusion = f32[1024,128]{0,1:T(8,128)S(1)} fusion(f32[16,8,64,1024]{3,2,1,0:T(8,128)S(1)} %copy.11), kind=kLoop, calls=%fused_computation | loop fusion | flops 8257536 | bytes 34078720 | tf_op jit(solution)/shard_map/reduce_sum | solution.py:72
  284.3 5.5 %convolution_subtract_fusion = f32[128,6,480]{0,2,1:T(8,128)} fusion(bf16[1024,6,480]{0,2,1:T(8,128)(2,1)} %all-gather.4.cloned.1.call-done, f32[128,6,480]{0,2,1:T(8,128)S(1)} %copy-done, f32[128,6,480]{0,2,1:T(8,128)S(1)} %get-tuple-element.3, f32[6,480]{1,0:T(8,128)S(1)} %copy-done.1, f32[1024,128]{0,1:T(8,128)S(1)} %bitcast_reduce_fusion), kind=kOutput, calls=%fused_computation.42 | convolution fusion | flops 756342784 | bytes 10857728 | tf_op jit(solution)/shard_map/or,oyc->ryc/dot_general | solution.py:75
  (10 shorter events, 0.1 us)
Async XLA Ops:
  7.2 85.2 %all-gather.4.cloned.1.call-start = ((), (), s32[]{:S(2)}) async-start(), calls=%async_computation | async-start | bytes 6635520 | tf_op jit(solution)/shard_map/all_gather | solution.py:68
  7.9 8.7 %copy-start = (f32[128,6,480]{0,2,1:T(8,128)S(1)}, f32[128,6,480]{0,2,1:T(8,128)}, u32[]{:S(2)}) copy-start(f32[128,6,480]{0,2,1:T(8,128)} %param.6) | copy-start | bytes 4423684
  7.9 241.4 %all-gather.6.cloned.1.call-start = ((), (), s32[]{:S(2)}) async-start(), calls=%async_computation.1 | async-start | bytes 34078720 | tf_op jit(solution)/shard_map/all_gather | solution.py:72
  9.7 39.4 %collective-permute-start.2 = (f32[128,6,320]{0,2,1:T(8,128)S(1)}, f32[128,6,320]{0,2,1:T(8,128)S(1)}, u32[]{:S(2)}, u32[]{:S(2)}) collective-permute-start(f32[128,6,320]{0,2,1:T(8,128)S(1)} %get-tuple-element.42), channel_id=1, source_target_pairs={{1,0},{2,1},{3,2},{4,3},{5,4},{6,5},{7,6},{0,7},{9,8},{10,9},{11,1... | collective-permute-start | bytes 2949128 | tf_op jit(solution)/shard_map/ppermute | solution.py:19
  16.6 27.3 %collective-permute-start.3 = (f32[128,6,320]{0,2,1:T(8,128)S(1)}, f32[128,6,320]{0,2,1:T(8,128)S(1)}, u32[]{:S(2)}, u32[]{:S(2)}) collective-permute-start(f32[128,6,320]{0,2,1:T(8,128)S(1)} %get-tuple-element.43), channel_id=1, source_target_pairs={{0,1},{1,2},{2,3},{3,4},{4,5},{5,6},{6,7},{7,0},{8,9},{9,10},{10,1... | collective-permute-start | bytes 2949128 | tf_op jit(solution)/shard_map/ppermute | solution.py:16
  16.7 32.2 %collective-permute-start = (f32[128,4,480]{0,2,1:T(8,128)S(1)}, f32[128,4,480]{0,2,1:T(8,128)S(1)}, u32[]{:S(2)}, u32[]{:S(2)}) collective-permute-start(f32[128,4,480]{0,2,1:T(8,128)S(1)} %get-tuple-element.36), channel_id=1, source_target_pairs={{8,0},{16,8},{24,16},{32,24},{40,32},{48,40},{56,48},{0,56},{9,1},... | collective-permute-start | bytes 2949128 | tf_op jit(solution)/shard_map/ppermute | solution.py:19
  23.2 25.1 %collective-permute-start.1 = (f32[128,4,480]{0,2,1:T(8,128)S(1)}, f32[128,4,480]{0,2,1:T(8,128)S(1)}, u32[]{:S(2)}, u32[]{:S(2)}) collective-permute-start(f32[128,4,480]{0,2,1:T(8,128)S(1)} %get-tuple-element.37), channel_id=1, source_target_pairs={{0,8},{8,16},{16,24},{24,32},{32,40},{40,48},{48,56},{56,0},{1,9},... | collective-permute-start | bytes 2949128 | tf_op jit(solution)/shard_map/ppermute | solution.py:16
  49.0 0.7 copy-start.2
  49.1 0.7 copy-start.3
  49.8 42.6 %copy-start.1 = (f32[6,480]{1,0:T(8,128)S(1)}, f32[6,480]{1,0:T(8,128)}, u32[]{:S(2)}) copy-start(f32[6,480]{1,0:T(8,128)} %param.11) | copy-start | bytes 34564
  92.4 5.2 %copy-start.4 = (f32[128]{0:T(128)S(1)}, f32[128]{0:T(128)}, u32[]{:S(2)}) copy-start(f32[128]{0:T(128)} %get-tuple-element.2) | copy-start | bytes 1540
Sparse Core Ops, SparseCore 0:
  10.0 82.3 all-gather.3
  97.7 151.5 all-gather.5
